TPU v7x, 32 devices: a whole 2x2x4 slice. The times are simulated.
32 devices in a mesh: groups: 2 (over y), section: 4 (over x, core), dp: 4 (over z).
Axes of the slice: x: 2, y: 2, z: 4, core: 2. Of those that a mesh axis runs over, the one named last changes fastest.
Arguments:
- patches: bfloat16 [8192, 1024], P(('groups', 'dp'), 'section'), parts along dimension 0, may hold values from -6 to 6
- clip_slot: int32 [256], P('groups'), parts along dimension 0, may hold values from 0 to 127, each once
- w_qkv: bfloat16 [4, 1024, 1536], P('section'), may hold values from -0.1875 to 0.1875
- w_out: bfloat16 [4, 512, 1024], P('section'), may hold values from -0.25 to 0.25
- w_up: bfloat16 [4, 1024, 2048], P('section'), may hold values from -0.1875 to 0.1875
- w_down: bfloat16 [4, 2048, 1024], P('section'), may hold values from -0.125 to 0.125
- norm_gains: float32 [4, 2, 1024], P('section'), may hold values from 0.5 to 1.5
- level_one_weight: bfloat16 [3, 1024, 1024], P(None, 'section'), may hold values from -0.109375 to 0.109375
- level_two_weight: bfloat16 [3, 1024, 1024], P(None, 'section'), may hold values from -0.109375 to 0.109375
- head_weight: bfloat16 [1024, 22], P('section'), may hold values from -0.1875 to 0.1875
Outputs:
- level_one_heads: float32 [256, 22], P(('groups', 'dp')), parts along dimension 0
- level_two_heads: float32 [128, 22], P(('groups', 'dp')), parts along dimension 0
There are 2 independent parts, one for each index of `groups`. A program takes and returns all parts, laid end to end along the dimension named above; an argument that names none is the same for every part. Nothing has to cross between parts.
Inputs may be any that keep to these rules, and one draw needn't show every extreme that they name: clip_slot is a permutation: every slot of the window holds exactly one clip.
All inputs are finite; a program needn't handle non-finite values.
Results may differ from a plain program's by a relative error of at most 0.035.
Values may be sent and summed in bfloat16 or wider, within the bound.
A program may use at most 64 MiB of HBM per device.

v0:
```python
import jax
import jax.numpy as jnp
from jax import lax
from jax.sharding import PartitionSpec as P

HEADS = 8
HEAD = 64
PATCHES = 16
TUB_CLIP = 2


EPSILON = 1e-05


def shifted(value, axis, steps):
    count = lax.axis_size(axis)
    leading, last = (max(0, -steps), min(count, count - steps))
    return lax.ppermute(value, axis, [(source, source + steps) for source in range(leading, last)])


def broadcast(value, axis, source):
    kept = jnp.where(lax.axis_index(axis) == source, value, 0).astype(value.dtype)
    return lax.psum(kept, axis)


def layer_norm(values, scaling):
    average = jnp.mean(values, axis=-1, keepdims=True)
    centred = values - average
    spread = jnp.mean(centred * centred, axis=-1, keepdims=True)
    return centred * lax.rsqrt(spread + EPSILON) * scaling


def head_norm(values):
    return values * lax.rsqrt(jnp.mean(values * values, axis=-1, keepdims=True) + EPSILON)


def vit_layer(stream, w_qkv, w_out, w_up, w_down, gains, clip_tok, head_count, head_size):
    row_count = stream.shape[0]
    clip_count = row_count // clip_tok
    residual = stream.astype(jnp.float32)
    normed = layer_norm(residual, gains[0]).astype(jnp.bfloat16)
    projected = jnp.dot(normed, w_qkv, preferred_element_type=jnp.float32)
    projected = projected.reshape(clip_count, clip_tok, 3, head_count, head_size)
    queries = head_norm(projected[:, :, 0]).astype(jnp.bfloat16)
    key_rows = head_norm(projected[:, :, 1]).astype(jnp.bfloat16)
    value_rows = projected[:, :, 2].astype(jnp.bfloat16)
    scores = jnp.einsum(
        "cqhd,ckhd->chqk", queries, key_rows, preferred_element_type=jnp.float32
    ) * head_size ** (-0.5)
    exponent = jnp.exp(scores)
    attention_weights = (exponent / jnp.sum(exponent, axis=-1, keepdims=True)).astype(jnp.bfloat16)
    mixture = jnp.einsum(
        "chqk,ckhd->cqhd", attention_weights, value_rows, preferred_element_type=jnp.float32
    )
    mixture = mixture.astype(jnp.bfloat16).reshape(row_count, head_count * head_size)
    residual = residual + jnp.dot(mixture, w_out, preferred_element_type=jnp.float32)
    normed_b = layer_norm(residual, gains[1]).astype(jnp.bfloat16)
    hidden = jax.nn.gelu(
        jnp.dot(normed_b, w_up, preferred_element_type=jnp.float32), approximate=True
    ).astype(jnp.bfloat16)
    residual = residual + jnp.dot(hidden, w_down, preferred_element_type=jnp.float32)
    return residual.astype(jnp.bfloat16)


def conv_terms(padded_rows, weight_local, out_rows):
    picked = [padded_rows[offset : offset + 2 * out_rows - 1 : 2] for offset in range(3)]
    stacked = jnp.concatenate(picked, axis=1)
    flat_weight = weight_local.reshape(3 * weight_local.shape[1], weight_local.shape[2])
    return jnp.dot(stacked, flat_weight, preferred_element_type=jnp.float32)


def on_device(
    patches,
    clip_slot,
    w_qkv,
    w_out,
    w_up,
    w_down,
    norm_gains,
    level_one_weight,
    level_two_weight,
    head_weight,
):
    sections = lax.axis_size("section")
    section_index = lax.axis_index("section")
    shard_index = lax.axis_index("dp")
    gathered = lax.all_gather(patches, "section", axis=1, tiled=True)
    width = gathered.shape[1]
    clip_tok = TUB_CLIP * PATCHES
    clips_dev = gathered.shape[0] // clip_tok
    per_unit = 2
    unit_rows = per_unit * clip_tok
    unit_count = clips_dev // per_unit
    tubes_unit = per_unit * TUB_CLIP
    layer_weights = (w_qkv[0], w_out[0], w_up[0], w_down[0], norm_gains[0])

    def run_layer(block_rows):
        return vit_layer(block_rows, *layer_weights, clip_tok, HEADS, HEAD)

    def pass_through(block_rows):
        return block_rows

    def advance(moment, carried):
        outgoing, pooled = carried
        arrived = shifted(outgoing, "section", 1)
        fresh_rows = lax.dynamic_slice_in_dim(
            gathered, jnp.minimum(moment, unit_count - 1) * unit_rows, unit_rows, 0
        )
        incoming = jnp.where(section_index == 0, fresh_rows, arrived)
        unit_index = moment - section_index
        active = (unit_index >= 0) & (unit_index < unit_count)
        result = lax.cond(active, run_layer, pass_through, incoming)
        tube_means = jnp.mean(
            result.astype(jnp.float32).reshape(tubes_unit, PATCHES, width), axis=1
        )
        tube_start = jnp.clip(unit_index, 0, unit_count - 1) * tubes_unit
        current = lax.dynamic_slice_in_dim(pooled, tube_start, tubes_unit, 0)
        record_here = active & (section_index == sections - 1)
        pooled = lax.dynamic_update_slice_in_dim(
            pooled, jnp.where(record_here, tube_means, current), tube_start, 0
        )
        return (result, pooled)

    empty_rows = jnp.zeros((unit_rows, width), jnp.bfloat16)
    empty_pool = jnp.zeros((clips_dev * TUB_CLIP, width), jnp.float32)
    final_rows, pooled = lax.fori_loop(
        0, unit_count + sections - 1, advance, (empty_rows, empty_pool)
    )
    pooled = broadcast(pooled.astype(jnp.bfloat16), "section", sections - 1)
    local_positions = pooled.shape[0]
    film_position = (
        clip_slot[:, None] * TUB_CLIP + jnp.arange(TUB_CLIP, dtype=jnp.int32)[None, :]
    ).reshape(-1)
    targets = shard_index * local_positions + jnp.arange(local_positions, dtype=jnp.int32)
    selector = (targets[:, None] == film_position[None, :]).astype(jnp.bfloat16)
    film_rows = jnp.dot(
        selector,
        lax.all_gather(pooled, "dp", axis=0, tiled=True),
        preferred_element_type=jnp.float32,
    )
    film_rows = film_rows.astype(jnp.bfloat16)
    channels = width // sections
    chan_start = section_index * channels
    input_share = lax.dynamic_slice_in_dim(film_rows, chan_start, channels, 1)
    level_one_rows = local_positions // 2
    edge_input = shifted(input_share[-3:], "dp", 1)
    one_rows = level_one_rows + 1
    padded_input = jnp.concatenate([edge_input, input_share], axis=0)
    one_partial = conv_terms(padded_input, level_one_weight, one_rows)
    one_total = lax.psum(one_partial.astype(jnp.bfloat16), "section").astype(jnp.float32)
    one_total = lax.dynamic_slice_in_dim(one_total, chan_start, channels, 1)
    one_share = jax.nn.gelu(one_total, approximate=True).astype(jnp.bfloat16)
    level_one_out = one_share[1:]
    two_partial = conv_terms(one_share, level_two_weight, level_one_rows // 2)
    two_total = lax.psum(two_partial.astype(jnp.bfloat16), "section").astype(jnp.float32)
    two_total = lax.dynamic_slice_in_dim(two_total, chan_start, channels, 1)
    two_share = jax.nn.gelu(two_total, approximate=True).astype(jnp.bfloat16)
    head_one = jnp.dot(level_one_out, head_weight, preferred_element_type=jnp.float32)
    head_two = jnp.dot(two_share, head_weight, preferred_element_type=jnp.float32)
    head_one, head_two = lax.psum((head_one, head_two), "section")
    return (head_one, head_two)


def solution(mesh):
    return jax.shard_map(
        on_device,
        mesh=mesh,
        in_specs=(
            P(("groups", "dp"), "section"),
            P("groups"),
            P("section", None, None),
            P("section", None, None),
            P("section", None, None),
            P("section", None, None),
            P("section", None, None),
            P(None, "section", None),
            P(None, "section", None),
            P("section", None),
        ),
        out_specs=(P(("groups", "dp"), None), P(("groups", "dp"), None)),
        check_vma=False,
    )
```

profile of v0, /device:TPU:0, one launch (start us, length us, event | category | flops | bytes accessed | tf_op | source)
XLA Modules:
  0.0 553.1 jit_solution(6364947643892078391)
XLA Ops:
  9.4 25.7 %all-gather.2.cloned.1.call-done = bf16[1024,1024]{1,0:T(8,128)(2,1)} async-done(((bf16[1024,256]{1,0:T(8,128)(2,1)}), bf16[1024,1024]{1,0:T(8,128)(2,1)}) %all-gather.2.cloned.1.call-update) | async-done | bytes 2097168 | tf_op jit(solution)/shard_map/all_gather | solution.py:87
  35.8 372.3 %while.16 = (s32[]{:T(128)}, bf16[64,1024]{1,0:T(8,128)(2,1)S(1)}, bf16[64,1024]{1,0:T(8,128)(2,1)}, s32[]{:T(128)}, pred[]{:T(512)}, /*index=5*/bf16[1024,1024]...) while((s32[]{:T(128)}, bf16[64,1024]{1,0:T(8,128)(2,1)S(1)}, ...), condition=%wide.region_12.13_spmd, body=%wide.region_0.12_spmd.sunk | while | flops 812734080 | bytes 22180840 | solution.py:126
  39.9 13.1 %conditional.2 = (bf16[64,1024]{1,0:T(8,128)(2,1)S(1)}, f32[4,1024]{1,0:T(4,128)S(1)}) conditional(s32[]{:T(128)} %convert_element_type.183, bf16[64,1024]{1,0:T(8,128)(2,1)S(1)} %dynamic-slice_select_fusion.2, (bf16[64,1024]{1,0:T(8,128)(2,1)S(1)}, f32[2,1024]{1,0:T(2,128)}, bf16[1024,1536]{1,0:T(8,128)(2,1)}, bf16[512,1024]{1,0:T(8,128)(2,1)}, ...), branch_computations={%region_1.0_spmd, %region_3.11_spmd} | conditional | flops 812660352 | bytes 21230124 | solution.py:112
  57.5 13.1 %conditional.2 = (bf16[64,1024]{1,0:T(8,128)(2,1)S(1)}, f32[4,1024]{1,0:T(4,128)S(1)}) conditional(s32[]{:T(128)} %convert_element_type.183, bf16[64,1024]{1,0:T(8,128)(2,1)S(1)} %dynamic-slice_select_fusion.2, (bf16[64,1024]{1,0:T(8,128)(2,1)S(1)}, f32[2,1024]{1,0:T(2,128)}, bf16[1024,1536]{1,0:T(8,128)(2,1)}, bf16[512,1024]{1,0:T(8,128)(2,1)}, ...), branch_computations={%region_1.0_spmd, %region_3.11_spmd} | conditional | flops 812660352 | bytes 21230124 | solution.py:112
  76.1 13.1 %conditional.2 = (bf16[64,1024]{1,0:T(8,128)(2,1)S(1)}, f32[4,1024]{1,0:T(4,128)S(1)}) conditional(s32[]{:T(128)} %convert_element_type.183, bf16[64,1024]{1,0:T(8,128)(2,1)S(1)} %dynamic-slice_select_fusion.2, (bf16[64,1024]{1,0:T(8,128)(2,1)S(1)}, f32[2,1024]{1,0:T(2,128)}, bf16[1024,1536]{1,0:T(8,128)(2,1)}, bf16[512,1024]{1,0:T(8,128)(2,1)}, ...), branch_computations={%region_1.0_spmd, %region_3.11_spmd} | conditional | flops 812660352 | bytes 21230124 | solution.py:112
  95.2 13.1 %conditional.2 = (bf16[64,1024]{1,0:T(8,128)(2,1)S(1)}, f32[4,1024]{1,0:T(4,128)S(1)}) conditional(s32[]{:T(128)} %convert_element_type.183, bf16[64,1024]{1,0:T(8,128)(2,1)S(1)} %dynamic-slice_select_fusion.2, (bf16[64,1024]{1,0:T(8,128)(2,1)S(1)}, f32[2,1024]{1,0:T(2,128)}, bf16[1024,1536]{1,0:T(8,128)(2,1)}, bf16[512,1024]{1,0:T(8,128)(2,1)}, ...), branch_computations={%region_1.0_spmd, %region_3.11_spmd} | conditional | flops 812660352 | bytes 21230124 | solution.py:112
  109.7 5.3 collective-permute-start
  116.9 13.1 %conditional.2 = (bf16[64,1024]{1,0:T(8,128)(2,1)S(1)}, f32[4,1024]{1,0:T(4,128)S(1)}) conditional(s32[]{:T(128)} %convert_element_type.183, bf16[64,1024]{1,0:T(8,128)(2,1)S(1)} %dynamic-slice_select_fusion.2, (bf16[64,1024]{1,0:T(8,128)(2,1)S(1)}, f32[2,1024]{1,0:T(2,128)}, bf16[1024,1536]{1,0:T(8,128)(2,1)}, bf16[512,1024]{1,0:T(8,128)(2,1)}, ...), branch_computations={%region_1.0_spmd, %region_3.11_spmd} | conditional | flops 812660352 | bytes 21230124 | solution.py:112
  138.5 13.1 %conditional.2 = (bf16[64,1024]{1,0:T(8,128)(2,1)S(1)}, f32[4,1024]{1,0:T(4,128)S(1)}) conditional(s32[]{:T(128)} %convert_element_type.183, bf16[64,1024]{1,0:T(8,128)(2,1)S(1)} %dynamic-slice_select_fusion.2, (bf16[64,1024]{1,0:T(8,128)(2,1)S(1)}, f32[2,1024]{1,0:T(2,128)}, bf16[1024,1536]{1,0:T(8,128)(2,1)}, bf16[512,1024]{1,0:T(8,128)(2,1)}, ...), branch_computations={%region_1.0_spmd, %region_3.11_spmd} | conditional | flops 812660352 | bytes 21230124 | solution.py:112
  152.9 5.3 collective-permute-start
  160.1 13.1 %conditional.2 = (bf16[64,1024]{1,0:T(8,128)(2,1)S(1)}, f32[4,1024]{1,0:T(4,128)S(1)}) conditional(s32[]{:T(128)} %convert_element_type.183, bf16[64,1024]{1,0:T(8,128)(2,1)S(1)} %dynamic-slice_select_fusion.2, (bf16[64,1024]{1,0:T(8,128)(2,1)S(1)}, f32[2,1024]{1,0:T(2,128)}, bf16[1024,1536]{1,0:T(8,128)(2,1)}, bf16[512,1024]{1,0:T(8,128)(2,1)}, ...), branch_computations={%region_1.0_spmd, %region_3.11_spmd} | conditional | flops 812660352 | bytes 21230124 | solution.py:112
  174.5 5.3 collective-permute-start
  181.8 13.1 %conditional.2 = (bf16[64,1024]{1,0:T(8,128)(2,1)S(1)}, f32[4,1024]{1,0:T(4,128)S(1)}) conditional(s32[]{:T(128)} %convert_element_type.183, bf16[64,1024]{1,0:T(8,128)(2,1)S(1)} %dynamic-slice_select_fusion.2, (bf16[64,1024]{1,0:T(8,128)(2,1)S(1)}, f32[2,1024]{1,0:T(2,128)}, bf16[1024,1536]{1,0:T(8,128)(2,1)}, bf16[512,1024]{1,0:T(8,128)(2,1)}, ...), branch_computations={%region_1.0_spmd, %region_3.11_spmd} | conditional | flops 812660352 | bytes 21230124 | solution.py:112
  203.4 13.1 %conditional.2 = (bf16[64,1024]{1,0:T(8,128)(2,1)S(1)}, f32[4,1024]{1,0:T(4,128)S(1)}) conditional(s32[]{:T(128)} %convert_element_type.183, bf16[64,1024]{1,0:T(8,128)(2,1)S(1)} %dynamic-slice_select_fusion.2, (bf16[64,1024]{1,0:T(8,128)(2,1)S(1)}, f32[2,1024]{1,0:T(2,128)}, bf16[1024,1536]{1,0:T(8,128)(2,1)}, bf16[512,1024]{1,0:T(8,128)(2,1)}, ...), branch_computations={%region_1.0_spmd, %region_3.11_spmd} | conditional | flops 812660352 | bytes 21230124 | solution.py:112
  217.8 5.3 collective-permute-start
  225.0 13.1 %conditional.2 = (bf16[64,1024]{1,0:T(8,128)(2,1)S(1)}, f32[4,1024]{1,0:T(4,128)S(1)}) conditional(s32[]{:T(128)} %convert_element_type.183, bf16[64,1024]{1,0:T(8,128)(2,1)S(1)} %dynamic-slice_select_fusion.2, (bf16[64,1024]{1,0:T(8,128)(2,1)S(1)}, f32[2,1024]{1,0:T(2,128)}, bf16[1024,1536]{1,0:T(8,128)(2,1)}, bf16[512,1024]{1,0:T(8,128)(2,1)}, ...), branch_computations={%region_1.0_spmd, %region_3.11_spmd} | conditional | flops 812660352 | bytes 21230124 | solution.py:112
  246.6 13.1 %conditional.2 = (bf16[64,1024]{1,0:T(8,128)(2,1)S(1)}, f32[4,1024]{1,0:T(4,128)S(1)}) conditional(s32[]{:T(128)} %convert_element_type.183, bf16[64,1024]{1,0:T(8,128)(2,1)S(1)} %dynamic-slice_select_fusion.2, (bf16[64,1024]{1,0:T(8,128)(2,1)S(1)}, f32[2,1024]{1,0:T(2,128)}, bf16[1024,1536]{1,0:T(8,128)(2,1)}, bf16[512,1024]{1,0:T(8,128)(2,1)}, ...), branch_computations={%region_1.0_spmd, %region_3.11_spmd} | conditional | flops 812660352 | bytes 21230124 | solution.py:112
  268.3 13.1 %conditional.2 = (bf16[64,1024]{1,0:T(8,128)(2,1)S(1)}, f32[4,1024]{1,0:T(4,128)S(1)}) conditional(s32[]{:T(128)} %convert_element_type.183, bf16[64,1024]{1,0:T(8,128)(2,1)S(1)} %dynamic-slice_select_fusion.2, (bf16[64,1024]{1,0:T(8,128)(2,1)S(1)}, f32[2,1024]{1,0:T(2,128)}, bf16[1024,1536]{1,0:T(8,128)(2,1)}, bf16[512,1024]{1,0:T(8,128)(2,1)}, ...), branch_computations={%region_1.0_spmd, %region_3.11_spmd} | conditional | flops 812660352 | bytes 21230124 | solution.py:112
  282.7 5.3 collective-permute-start
  289.9 13.1 %conditional.2 = (bf16[64,1024]{1,0:T(8,128)(2,1)S(1)}, f32[4,1024]{1,0:T(4,128)S(1)}) conditional(s32[]{:T(128)} %convert_element_type.183, bf16[64,1024]{1,0:T(8,128)(2,1)S(1)} %dynamic-slice_select_fusion.2, (bf16[64,1024]{1,0:T(8,128)(2,1)S(1)}, f32[2,1024]{1,0:T(2,128)}, bf16[1024,1536]{1,0:T(8,128)(2,1)}, bf16[512,1024]{1,0:T(8,128)(2,1)}, ...), branch_computations={%region_1.0_spmd, %region_3.11_spmd} | conditional | flops 812660352 | bytes 21230124 | solution.py:112
  304.3 5.3 collective-permute-start
  311.5 13.1 %conditional.2 = (bf16[64,1024]{1,0:T(8,128)(2,1)S(1)}, f32[4,1024]{1,0:T(4,128)S(1)}) conditional(s32[]{:T(128)} %convert_element_type.183, bf16[64,1024]{1,0:T(8,128)(2,1)S(1)} %dynamic-slice_select_fusion.2, (bf16[64,1024]{1,0:T(8,128)(2,1)S(1)}, f32[2,1024]{1,0:T(2,128)}, bf16[1024,1536]{1,0:T(8,128)(2,1)}, bf16[512,1024]{1,0:T(8,128)(2,1)}, ...), branch_computations={%region_1.0_spmd, %region_3.11_spmd} | conditional | flops 812660352 | bytes 21230124 | solution.py:112
  325.9 5.3 collective-permute-start
  333.1 13.1 %conditional.2 = (bf16[64,1024]{1,0:T(8,128)(2,1)S(1)}, f32[4,1024]{1,0:T(4,128)S(1)}) conditional(s32[]{:T(128)} %convert_element_type.183, bf16[64,1024]{1,0:T(8,128)(2,1)S(1)} %dynamic-slice_select_fusion.2, (bf16[64,1024]{1,0:T(8,128)(2,1)S(1)}, f32[2,1024]{1,0:T(2,128)}, bf16[1024,1536]{1,0:T(8,128)(2,1)}, bf16[512,1024]{1,0:T(8,128)(2,1)}, ...), branch_computations={%region_1.0_spmd, %region_3.11_spmd} | conditional | flops 812660352 | bytes 21230124 | solution.py:112
  347.5 5.3 collective-permute-start
  354.8 13.1 %conditional.2 = (bf16[64,1024]{1,0:T(8,128)(2,1)S(1)}, f32[4,1024]{1,0:T(4,128)S(1)}) conditional(s32[]{:T(128)} %convert_element_type.183, bf16[64,1024]{1,0:T(8,128)(2,1)S(1)} %dynamic-slice_select_fusion.2, (bf16[64,1024]{1,0:T(8,128)(2,1)S(1)}, f32[2,1024]{1,0:T(2,128)}, bf16[1024,1536]{1,0:T(8,128)(2,1)}, bf16[512,1024]{1,0:T(8,128)(2,1)}, ...), branch_computations={%region_1.0_spmd, %region_3.11_spmd} | conditional | flops 812660352 | bytes 21230124 | solution.py:112
  377.8 18.3 %collective-permute-start = (bf16[64,1024]{1,0:T(8,128)(2,1)S(1)}, bf16[64,1024]{1,0:T(8,128)(2,1)S(1)}, u32[]{:S(2)}, u32[]{:S(2)}) collective-permute-start(bf16[64,1024]{1,0:T(8,128)(2,1)S(1)} %get-tuple-element.386), channel_id=1, source_target_pairs={{0,4},{4,8},{8,12},{1,5},{5,9},{9,13},{2,6},{6,10},{10,14},{3,7},{... | collective-permute-start | bytes 393224 | tf_op jit(solution)/shard_map/while/body/eval_jaxpr/ppermute | solution.py:18
  408.8 60.7 %all-reduce.4.cloned.1.call-done = bf16[64,1024]{1,0:T(8,128)(2,1)} async-done(((bf16[64,1024]{1,0:T(8,128)(2,1)}), bf16[64,1024]{1,0:T(8,128)(2,1)}) %all-reduce.4.cloned.1.call-update) | async-done | bytes 131088 | tf_op jit(solution)/shard_map/psum | solution.py:23
  469.5 14.9 %all_gather.7 = bf16[256,1024]{1,0:T(8,128)(2,1)S(1)} all-gather(bf16[64,1024]{1,0:T(8,128)(2,1)} %all-reduce.4.cloned.1.call-done), channel_id=1, replica_groups=mesh['groups'=2,'section'=4,'dp'=4] {'dp'}, dimensions={0}, use_global_device_ids=true | all-gather | bytes 655360 | tf_op jit(solution)/shard_map/all_gather | solution.py:138
  491.8 31.6 %all-reduce.6.cloned.1.call-done = bf16[33,1024]{1,0:T(8,128)(2,1)} async-done(((bf16[33,1024]{1,0:T(8,128)(2,1)}), bf16[33,1024]{1,0:T(8,128)(2,1)}) %all-reduce.6.cloned.1.call-update) | async-done | bytes 67600 | tf_op jit(solution)/shard_map/psum | solution.py:150
  524.6 10.7 %psum.38 = bf16[16,1024]{1,0:T(8,128)(2,1)S(1)} all-reduce(bf16[16,1024]{1,0:T(8,128)(2,1)S(1)} %convolution_convert_fusion.2), channel_id=1, replica_groups=mesh['groups'=2,'section'=4,'dp'=4] {'section'}, use_global_device_ids=true, to_apply=%region_16.17 | all-reduce | flops 16384 | bytes 65536 | tf_op jit(solution)/shard_map/psum | solution.py:155
  535.4 11.1 %all-reduce = (f32[32,22]{0,1:T(8,128)}, f32[16,22]{1,0:T(8,128)}) all-reduce(f32[32,22]{0,1:T(8,128)S(1)} %fusion.70, f32[16,22]{1,0:T(8,128)S(1)} %fusion.72), channel_id=1, replica_groups=mesh['groups'=2,'section'=4,'dp'=4] {'section'}, use_global_device_ids=true, to_apply=%region_15.16 | all-reduce | flops 1056 | bytes 8448 | tf_op jit(solution)/shard_map/psum | solution.py:160
  (477 shorter events, 321.3 us)
Async XLA Ops:
  7.2 483.6 %copy-start = (bf16[3,256,1024]{2,1,0:T(8,128)(2,1)S(1)}, bf16[3,256,1024]{2,1,0:T(8,128)(2,1)}, u32[]{:S(2)}) copy-start(bf16[3,256,1024]{2,1,0:T(8,128)(2,1)} %param.21) | copy-start | bytes 4718596
  7.2 27.9 %all-gather.2.cloned.1.call-start = ((), (), s32[]{:S(2)}) async-start(), calls=%async_computation | async-start | bytes 2621440 | tf_op jit(solution)/shard_map/all_gather | solution.py:87
  7.9 461.6 %all-reduce.4.cloned.1.call-start = ((), (), s32[]{:S(2)}) async-start(), calls=%async_computation.1 | async-start | bytes 262144 | tf_op jit(solution)/shard_map/psum | solution.py:23
  35.8 3.1 collective-permute-start
  44.4 2.7 copy-start.1
  54.3 2.3 collective-permute-start
  62.0 2.7 copy-start.1
  71.9 3.2 collective-permute-start
  90.5 3.8 collective-permute-start
  109.7 6.3 %collective-permute-start = (bf16[64,1024]{1,0:T(8,128)(2,1)S(1)}, bf16[64,1024]{1,0:T(8,128)(2,1)S(1)}, u32[]{:S(2)}, u32[]{:S(2)}) collective-permute-start(bf16[64,1024]{1,0:T(8,128)(2,1)S(1)} %get-tuple-element.386), channel_id=1, source_target_pairs={{0,4},{4,8},{8,12},{1,5},{5,9},{9,13},{2,6},{6,10},{10,14},{3,7},{... | collective-permute-start | bytes 393224 | tf_op jit(solution)/shard_map/while/body/eval_jaxpr/ppermute | solution.py:18
  131.3 6.3 %collective-permute-start = (bf16[64,1024]{1,0:T(8,128)(2,1)S(1)}, bf16[64,1024]{1,0:T(8,128)(2,1)S(1)}, u32[]{:S(2)}, u32[]{:S(2)}) collective-permute-start(bf16[64,1024]{1,0:T(8,128)(2,1)S(1)} %get-tuple-element.386), channel_id=1, source_target_pairs={{0,4},{4,8},{8,12},{1,5},{5,9},{9,13},{2,6},{6,10},{10,14},{3,7},{... | collective-permute-start | bytes 393224 | tf_op jit(solution)/shard_map/while/body/eval_jaxpr/ppermute | solution.py:18
  143.0 2.7 copy-start.1
  152.9 6.3 %collective-permute-start = (bf16[64,1024]{1,0:T(8,128)(2,1)S(1)}, bf16[64,1024]{1,0:T(8,128)(2,1)S(1)}, u32[]{:S(2)}, u32[]{:S(2)}) collective-permute-start(bf16[64,1024]{1,0:T(8,128)(2,1)S(1)} %get-tuple-element.386), channel_id=1, source_target_pairs={{0,4},{4,8},{8,12},{1,5},{5,9},{9,13},{2,6},{6,10},{10,14},{3,7},{... | collective-permute-start | bytes 393224 | tf_op jit(solution)/shard_map/while/body/eval_jaxpr/ppermute | solution.py:18
  174.5 6.3 %collective-permute-start = (bf16[64,1024]{1,0:T(8,128)(2,1)S(1)}, bf16[64,1024]{1,0:T(8,128)(2,1)S(1)}, u32[]{:S(2)}, u32[]{:S(2)}) collective-permute-start(bf16[64,1024]{1,0:T(8,128)(2,1)S(1)} %get-tuple-element.386), channel_id=1, source_target_pairs={{0,4},{4,8},{8,12},{1,5},{5,9},{9,13},{2,6},{6,10},{10,14},{3,7},{... | collective-permute-start | bytes 393224 | tf_op jit(solution)/shard_map/while/body/eval_jaxpr/ppermute | solution.py:18
  186.3 2.7 copy-start.1
  196.2 6.3 %collective-permute-start = (bf16[64,1024]{1,0:T(8,128)(2,1)S(1)}, bf16[64,1024]{1,0:T(8,128)(2,1)S(1)}, u32[]{:S(2)}, u32[]{:S(2)}) collective-permute-start(bf16[64,1024]{1,0:T(8,128)(2,1)S(1)} %get-tuple-element.386), channel_id=1, source_target_pairs={{0,4},{4,8},{8,12},{1,5},{5,9},{9,13},{2,6},{6,10},{10,14},{3,7},{... | collective-permute-start | bytes 393224 | tf_op jit(solution)/shard_map/while/body/eval_jaxpr/ppermute | solution.py:18
  207.9 2.7 copy-start.1
  217.8 6.3 %collective-permute-start = (bf16[64,1024]{1,0:T(8,128)(2,1)S(1)}, bf16[64,1024]{1,0:T(8,128)(2,1)S(1)}, u32[]{:S(2)}, u32[]{:S(2)}) collective-permute-start(bf16[64,1024]{1,0:T(8,128)(2,1)S(1)} %get-tuple-element.386), channel_id=1, source_target_pairs={{0,4},{4,8},{8,12},{1,5},{5,9},{9,13},{2,6},{6,10},{10,14},{3,7},{... | collective-permute-start | bytes 393224 | tf_op jit(solution)/shard_map/while/body/eval_jaxpr/ppermute | solution.py:18
  239.4 6.3 %collective-permute-start = (bf16[64,1024]{1,0:T(8,128)(2,1)S(1)}, bf16[64,1024]{1,0:T(8,128)(2,1)S(1)}, u32[]{:S(2)}, u32[]{:S(2)}) collective-permute-start(bf16[64,1024]{1,0:T(8,128)(2,1)S(1)} %get-tuple-element.386), channel_id=1, source_target_pairs={{0,4},{4,8},{8,12},{1,5},{5,9},{9,13},{2,6},{6,10},{10,14},{3,7},{... | collective-permute-start | bytes 393224 | tf_op jit(solution)/shard_map/while/body/eval_jaxpr/ppermute | solution.py:18
  261.0 6.3 %collective-permute-start = (bf16[64,1024]{1,0:T(8,128)(2,1)S(1)}, bf16[64,1024]{1,0:T(8,128)(2,1)S(1)}, u32[]{:S(2)}, u32[]{:S(2)}) collective-permute-start(bf16[64,1024]{1,0:T(8,128)(2,1)S(1)} %get-tuple-element.386), channel_id=1, source_target_pairs={{0,4},{4,8},{8,12},{1,5},{5,9},{9,13},{2,6},{6,10},{10,14},{3,7},{... | collective-permute-start | bytes 393224 | tf_op jit(solution)/shard_map/while/body/eval_jaxpr/ppermute | solution.py:18
  282.7 6.3 %collective-permute-start = (bf16[64,1024]{1,0:T(8,128)(2,1)S(1)}, bf16[64,1024]{1,0:T(8,128)(2,1)S(1)}, u32[]{:S(2)}, u32[]{:S(2)}) collective-permute-start(bf16[64,1024]{1,0:T(8,128)(2,1)S(1)} %get-tuple-element.386), channel_id=1, source_target_pairs={{0,4},{4,8},{8,12},{1,5},{5,9},{9,13},{2,6},{6,10},{10,14},{3,7},{... | collective-permute-start | bytes 393224 | tf_op jit(solution)/shard_map/while/body/eval_jaxpr/ppermute | solution.py:18
  294.4 2.7 copy-start.1
  304.3 6.3 %collective-permute-start = (bf16[64,1024]{1,0:T(8,128)(2,1)S(1)}, bf16[64,1024]{1,0:T(8,128)(2,1)S(1)}, u32[]{:S(2)}, u32[]{:S(2)}) collective-permute-start(bf16[64,1024]{1,0:T(8,128)(2,1)S(1)} %get-tuple-element.386), channel_id=1, source_target_pairs={{0,4},{4,8},{8,12},{1,5},{5,9},{9,13},{2,6},{6,10},{10,14},{3,7},{... | collective-permute-start | bytes 393224 | tf_op jit(solution)/shard_map/while/body/eval_jaxpr/ppermute | solution.py:18
  325.9 6.3 %collective-permute-start = (bf16[64,1024]{1,0:T(8,128)(2,1)S(1)}, bf16[64,1024]{1,0:T(8,128)(2,1)S(1)}, u32[]{:S(2)}, u32[]{:S(2)}) collective-permute-start(bf16[64,1024]{1,0:T(8,128)(2,1)S(1)} %get-tuple-element.386), channel_id=1, source_target_pairs={{0,4},{4,8},{8,12},{1,5},{5,9},{9,13},{2,6},{6,10},{10,14},{3,7},{... | collective-permute-start | bytes 393224 | tf_op jit(solution)/shard_map/while/body/eval_jaxpr/ppermute | solution.py:18
  347.5 6.3 %collective-permute-start = (bf16[64,1024]{1,0:T(8,128)(2,1)S(1)}, bf16[64,1024]{1,0:T(8,128)(2,1)S(1)}, u32[]{:S(2)}, u32[]{:S(2)}) collective-permute-start(bf16[64,1024]{1,0:T(8,128)(2,1)S(1)} %get-tuple-element.386), channel_id=1, source_target_pairs={{0,4},{4,8},{8,12},{1,5},{5,9},{9,13},{2,6},{6,10},{10,14},{3,7},{... | collective-permute-start | bytes 393224 | tf_op jit(solution)/shard_map/while/body/eval_jaxpr/ppermute | solution.py:18
  369.2 6.3 %collective-permute-start = (bf16[64,1024]{1,0:T(8,128)(2,1)S(1)}, bf16[64,1024]{1,0:T(8,128)(2,1)S(1)}, u32[]{:S(2)}, u32[]{:S(2)}) collective-permute-start(bf16[64,1024]{1,0:T(8,128)(2,1)S(1)} %get-tuple-element.386), channel_id=1, source_target_pairs={{0,4},{4,8},{8,12},{1,5},{5,9},{9,13},{2,6},{6,10},{10,14},{3,7},{... | collective-permute-start | bytes 393224 | tf_op jit(solution)/shard_map/while/body/eval_jaxpr/ppermute | solution.py:18
  377.8 19.3 %collective-permute-start = (bf16[64,1024]{1,0:T(8,128)(2,1)S(1)}, bf16[64,1024]{1,0:T(8,128)(2,1)S(1)}, u32[]{:S(2)}, u32[]{:S(2)}) collective-permute-start(bf16[64,1024]{1,0:T(8,128)(2,1)S(1)} %get-tuple-element.386), channel_id=1, source_target_pairs={{0,4},{4,8},{8,12},{1,5},{5,9},{9,13},{2,6},{6,10},{10,14},{3,7},{... | collective-permute-start | bytes 393224 | tf_op jit(solution)/shard_map/while/body/eval_jaxpr/ppermute | solution.py:18
  399.4 6.3 %collective-permute-start = (bf16[64,1024]{1,0:T(8,128)(2,1)S(1)}, bf16[64,1024]{1,0:T(8,128)(2,1)S(1)}, u32[]{:S(2)}, u32[]{:S(2)}) collective-permute-start(bf16[64,1024]{1,0:T(8,128)(2,1)S(1)} %get-tuple-element.386), channel_id=1, source_target_pairs={{0,4},{4,8},{8,12},{1,5},{5,9},{9,13},{2,6},{6,10},{10,14},{3,7},{... | collective-permute-start | bytes 393224 | tf_op jit(solution)/shard_map/while/body/eval_jaxpr/ppermute | solution.py:18
  408.0 116.1 %copy-start.3 = (bf16[256,22]{0,1:T(8,128)(2,1)S(1)}, bf16[256,22]{0,1:T(8,128)(2,1)}, u32[]{:S(2)}) copy-start(bf16[256,22]{0,1:T(8,128)(2,1)} %param.23) | copy-start | bytes 33796
  408.0 116.2 %copy-start.2 = (bf16[3,256,1024]{2,1,0:T(8,128)(2,1)S(1)}, bf16[3,256,1024]{2,1,0:T(8,128)(2,1)}, u32[]{:S(2)}) copy-start(bf16[3,256,1024]{2,1,0:T(8,128)(2,1)} %param.22) | copy-start | bytes 4718596
  408.7 114.6 %all-reduce.6.cloned.1.call-start = ((), (), s32[]{:S(2)}) async-start(), calls=%async_computation.2 | async-start | bytes 163840 | tf_op jit(solution)/shard_map/psum | solution.py:150
  485.3 5.3 collective-permute-start.1
  (10 other events, 26.6 us)
Sparse Core Ops, SparseCore 0:
  9.5 25.5 all-gather.1
  408.8 60.5 all-reduce.3
  491.9 31.3 all-reduce.5
where the time goes:
time: 557 us; the launch traced here: 553 us
  matrix products  158 us (28%)
  waiting for transfers between devices  138 us (25%)
  starting transfers between devices  105 us (19%)
  other arithmetic  57.8 us (10%)
  local copies, waits for them, and re-layouts  41 us (7%)
  blocking collectives  36.7 us (7%)
  between operations  13.9 us (2%)
    ppermute x20, starting transfers between devices, shifted(): lax.ppermute(value, axis, [(source, source + steps) for source in range(l...  105 us
    dot_general x16, matrix products, vit_layer(): jnp.dot(hidden, w_down, preferred_element_type=jnp.float32)  84.4 us
    psum x1, waiting for transfers between devices, broadcast(): return lax.psum(kept, axis)  60.7 us
    dot_general x16, matrix products, vit_layer(): projected = jnp.dot(normed, w_qkv, preferred_element_type=jnp.float32)  41.3 us
    psum x1, waiting for transfers between devices, on_device(): lax.psum(one_partial.astype(jnp.bfloat16), 'section').astype(jnp.float32)  31.6 us
    all_gather x1, waiting for transfers between devices, on_device(): gathered = lax.all_gather(patches, 'section', axis=1, tiled=True)  25.7 us
    dynamic_update_slice x19, other arithmetic, advance(): lax.dynamic_update_slice_in_dim(pooled, jnp.where(record_here, tube_means...  25.3 us
    slice x16, local copies, waits for them, and re-layouts, vit_layer(): normed_b = layer_norm(residual, gains[1]).astype(jnp.bfloat16)  22.1 us
  transfers between devices with their start and end apart: 23, of which 23 were waited for; matrix products, arithmetic and copies ran while one was open for 0% of the time, Pallas kernels for 0%

commit v1 on v0

v1 whole, which is shorter than its diff:
```python
import functools

import jax
import jax.numpy as jnp
from jax import lax
from jax.experimental import pallas as pl
from jax.experimental.pallas import tpu as pltpu
from jax.sharding import PartitionSpec as P

HEADS = 8
HEAD = 64
PATCHES = 16
TUB_CLIP = 2
EPSILON = 1e-05
UNIT_ROWS = 128
ROW_BLOCK = 128
CHUNK = 512
MESH = pl.DeviceIdType.MESH
F32 = jnp.float32
BF16 = jnp.bfloat16


def dot(a, b):
    return jnp.dot(a, b, preferred_element_type=F32)


def dot_nt(a, b):
    return lax.dot_general(a, b, (((1,), (1,)), ((), ())), preferred_element_type=F32)


def layer_norm(values, scaling):
    average = jnp.mean(values, axis=-1, keepdims=True)
    centred = values - average
    spread = jnp.mean(centred * centred, axis=-1, keepdims=True)
    return centred * lax.rsqrt(spread + EPSILON) * scaling


def gelu(values):
    return jax.nn.gelu(values, approximate=True)


def iota(shape, dim):
    return lax.broadcasted_iota(jnp.int32, shape, dim)


def head_scale(values):
    block = min(256, values.shape[1])
    same = iota((block, block), 0) // HEAD == iota((block, block), 1) // HEAD
    averaging = jnp.where(same, 1.0 / HEAD, 0.0).astype(BF16)
    squares = (values * values).astype(BF16)
    means = [
        dot(squares[:, start : start + block], averaging)
        for start in range(0, values.shape[1], block)
    ]
    return values * lax.rsqrt(jnp.concatenate(means, axis=1) + EPSILON)


def attention(queries, keys, values):
    clip = PATCHES * TUB_CLIP
    pair = 2 * HEAD
    rows = []
    cross = (2 * ROW_BLOCK, pair)
    own = (iota(cross, 0) < ROW_BLOCK) == (iota(cross, 1) < HEAD)
    own_bf = jnp.where(own, 1.0, 0.0).astype(BF16)
    square = (ROW_BLOCK, 2 * ROW_BLOCK)
    same_clip = iota(square, 0) // clip == (iota(square, 1) % ROW_BLOCK) // clip
    for start in range(0, queries.shape[0], ROW_BLOCK):
        mixed = []
        for lane in range(0, queries.shape[1], pair):
            q = queries[start : start + ROW_BLOCK, lane : lane + pair]
            k = keys[start : start + ROW_BLOCK, lane : lane + pair]
            v = values[start : start + ROW_BLOCK, lane : lane + pair]
            k2 = jnp.concatenate([k, k], axis=0) * own_bf
            v2 = jnp.concatenate([v, v], axis=0) * own_bf
            scores = dot_nt(q, k2)
            weights = jnp.where(same_clip, jnp.exp(scores), 0.0).astype(BF16)
            both = dot(weights, jnp.concatenate([v2, own_bf], axis=1))
            mixed.append((both[:, :pair] / both[:, pair:]).astype(BF16))
        rows.append(jnp.concatenate(mixed, axis=1))
    return jnp.concatenate(rows, axis=0) if len(rows) > 1 else rows[0]


def kernel(
    sections,
    shards,
    patches,
    clip_slot,
    w_qkv,
    w_out,
    w_up,
    w_down,
    gains,
    one_weight,
    two_weight,
    head_weight,
    head_one,
    head_two,
    v_qkv,
    v_out,
    v_up,
    v_down,
    v_one,
    v_two,
    gather,
    inbuf,
    outbuf,
    pooled_out,
    film_in,
    one_out,
    one_in,
    two_out,
    two_in,
    heads_out,
    heads_in,
    weight_sem,
    gather_send,
    gather_recv,
    hop_send,
    hop_recv,
    film_send,
    film_recv,
    ex_send,
    ex_recv,
):
    section = lax.axis_index("section")
    shard = lax.axis_index("dp")
    last = sections - 1
    units, unit_rows, width = inbuf.shape
    channels = width // sections
    tubes_unit = unit_rows // PATCHES
    hidden = v_up.shape[1]
    inner = v_out.shape[0]
    loads = [
        pltpu.make_async_copy(source, target, weight_sem.at[index])
        for index, (source, target) in enumerate(
            (
                (w_qkv.at[0], v_qkv),
                (w_out.at[0], v_out),
                (w_up.at[0], v_up),
                (w_down.at[0], v_down),
                (one_weight, v_one),
                (two_weight, v_two),
            )
        )
    ]
    for load in loads:
        load.start()

    barrier = pltpu.get_barrier_semaphore()
    for ds in range(sections):
        for dd in range(shards):
            if ds or dd:
                pl.semaphore_signal(
                    barrier,
                    inc=1,
                    device_id={
                        "section": lax.rem(section + ds, sections),
                        "dp": lax.rem(shard + dd, shards),
                    },
                    device_id_type=MESH,
                )
    pl.semaphore_wait(barrier, sections * shards - 1)

    def patch_rows(u):
        return pl.ds(pl.multiple_of(u * unit_rows, unit_rows), unit_rows)

    def patch_copy(u):
        return pltpu.make_async_remote_copy(
            src_ref=patches.at[patch_rows(u)],
            dst_ref=gather.at[section, u],
            send_sem=gather_send.at[u],
            recv_sem=gather_recv.at[section, u],
            device_id={"section": 0},
            device_id_type=MESH,
        )

    def patch_arrival(source, u):
        return pltpu.make_async_copy(
            patches.at[patch_rows(u)], gather.at[source, u], gather_recv.at[source, u]
        )

    def each_unit(body):
        def step(u, carry):
            body(u)
            return carry

        lax.fori_loop(0, units, step, 0)

    @pl.when(section > 0)
    def _():
        each_unit(lambda u: patch_copy(u).start())

    @pl.when(section == 0)
    def _():
        each_unit(lambda u: patch_arrival(0, u).start())

    def hop(u):
        return pltpu.make_async_remote_copy(
            src_ref=outbuf.at[u],
            dst_ref=inbuf.at[u],
            send_sem=hop_send.at[u],
            recv_sem=hop_recv.at[u],
            device_id={"section": lax.rem(section + 1, sections)},
            device_id_type=MESH,
        )

    def film_copy(u, target, step):
        return pltpu.make_async_remote_copy(
            src_ref=pooled_out.at[u, target],
            dst_ref=film_in.at[shard, u],
            send_sem=film_send.at[u, target, step],
            recv_sem=film_recv.at[shard, u],
            device_id={"section": target, "dp": lax.rem(shard + step, shards)},
            device_id_type=MESH,
        )

    film_targets = [
        (target, step)
        for target in range(sections)
        for step in range(shards)
        if not (target == last and step == 0)
    ]

    pooling_shape = (tubes_unit, unit_rows)
    pooling = jnp.where(
        iota(pooling_shape, 1) // PATCHES == iota(pooling_shape, 0), 1.0 / PATCHES, 0.0
    ).astype(BF16)

    def run_unit(u):
        @pl.when(section == 0)
        def _():
            for source in range(sections):
                patch_arrival(source, u).wait()
            inbuf[u] = jnp.concatenate([gather[source, u] for source in range(sections)], axis=1)

        @pl.when(section > 0)
        def _():
            hop(u).wait_recv()

        @pl.when(u == 0)
        def _():
            loads[0].wait()

        stream = inbuf[u].astype(F32)
        normed = layer_norm(stream, gains[0, 0:1]).astype(BF16)
        queries = (head_scale(dot(normed, v_qkv[:, :inner])) * HEAD**-0.5).astype(BF16)
        keys = head_scale(dot(normed, v_qkv[:, inner : 2 * inner])).astype(BF16)
        values = dot(normed, v_qkv[:, 2 * inner :]).astype(BF16)
        mixture = attention(queries, keys, values)

        @pl.when(u == 0)
        def _():
            loads[1].wait()
            loads[2].wait()
            loads[3].wait()

        residual = stream + dot(mixture, v_out[...])
        normed_b = layer_norm(residual, gains[0, 1:2]).astype(BF16)
        for start in range(0, hidden, CHUNK):
            part = gelu(dot(normed_b, v_up[:, start : start + CHUNK])).astype(BF16)
            residual = residual + dot(part, v_down[start : start + CHUNK, :])
        result = residual.astype(BF16)

        @pl.when(section < last)
        def _():
            outbuf[u] = result
            hop(u).start()

        @pl.when(section == last)
        def _():
            pooled = dot(pooling, result).astype(BF16).astype(F32)
            for target in range(sections):
                pooled_out[u, target] = pooled[:, target * channels : (target + 1) * channels]
            film_in[shard, u] = pooled[:, last * channels :]
            for target, step in film_targets:
                film_copy(u, target, step).start()

    each_unit(run_unit)

    loads[4].wait()
    loads[5].wait()

    def film_arrival(source, u):
        return pltpu.make_async_copy(
            film_in.at[source, u], film_in.at[source, u], film_recv.at[source, u]
        )

    @pl.when(section < last)
    def _():
        each_unit(lambda u: film_arrival(shard, u).wait())

    for step in range(1, shards):
        each_unit(lambda u: film_arrival(lax.rem(shard + step, shards), u).wait())

    tubes = shards * units * tubes_unit
    pooled = film_in[...].reshape(tubes, channels).astype(BF16)
    clips = tubes // TUB_CLIP
    spread_shape = (clips, tubes)
    spread = jnp.where(iota(spread_shape, 1) // TUB_CLIP == iota(spread_shape, 0), 1.0, 0.0)
    slots = jnp.broadcast_to(clip_slot[...].astype(F32), (8, clips)).astype(BF16)
    position = TUB_CLIP * dot(slots, spread.astype(BF16))[0:1]
    position = position + (iota((1, tubes), 1) % TUB_CLIP).astype(F32)

    two_rows = head_two.shape[0]
    one_rows = 3 * two_rows
    row = iota((one_rows, 1), 0)
    level_index = 2 * (shard * two_rows + row % two_rows) + row // two_rows - 1
    taps = []
    for tap in range(3):
        wanted = (2 * level_index + tap - 1).astype(F32)
        selector = jnp.where(position == wanted, 1.0, 0.0).astype(BF16)
        taps.append(dot(selector, pooled).astype(BF16))

    def conv(parts, weight):
        total = dot(parts[0], weight[0])
        for tap in (1, 2):
            total = total + dot(parts[tap], weight[tap])
        return total

    def exchange(stage, outgoing, incoming):
        copies = []
        for step in range(1, sections):
            target = lax.rem(section + step, sections)
            copies.append(
                pltpu.make_async_remote_copy(
                    src_ref=outgoing(target),
                    dst_ref=incoming.at[section],
                    send_sem=ex_send.at[stage, step],
                    recv_sem=ex_recv.at[stage, section],
                    device_id={"section": target},
                    device_id_type=MESH,
                )
            )
        for copy in copies:
            copy.start()

        def arrivals():
            for step in range(1, sections):
                source = lax.rem(section + step, sections)
                pltpu.make_async_copy(
                    incoming.at[source], incoming.at[source], ex_recv.at[stage, source]
                ).wait()
            for copy in copies:
                copy.wait_send()

        return arrivals

    def total(incoming):
        value = incoming[0].astype(F32)
        for source in range(1, sections):
            value = value + incoming[source].astype(F32)
        return value

    def scatter_sum(stage, partial, outgoing, incoming):
        partial = partial.astype(BF16)
        for target in range(sections):
            outgoing[target] = partial[:, target * channels : (target + 1) * channels]
        arrivals = exchange(stage, lambda target: outgoing.at[target], incoming)
        incoming[section] = outgoing[section]
        arrivals()
        return total(incoming)

    one = gelu(scatter_sum(0, conv(taps, v_one), one_out, one_in)).astype(BF16)
    parts = [one[block * two_rows : (block + 1) * two_rows] for block in range(3)]
    two_partial = conv(parts, v_two)
    two = gelu(scatter_sum(1, two_partial, two_out, two_in)).astype(BF16)

    natural = 2 * two_rows
    order = (natural, one_rows)
    chosen = iota(order, 1) == (1 + iota(order, 0) % 2) * two_rows + iota(order, 0) // 2
    one_natural = dot(jnp.where(chosen, 1.0, 0.0).astype(BF16), one).astype(BF16)
    outputs = head_weight.shape[1]
    heads_out[...] = jnp.zeros(heads_out.shape, F32)
    heads_out[0:natural, 0:outputs] = dot(one_natural, head_weight[...])
    heads_out[natural:, 0:outputs] = dot(two, head_weight[...])
    arrivals = exchange(2, lambda target: heads_out, heads_in)
    heads_in[section] = heads_out[...]
    arrivals()
    heads = total(heads_in)
    head_one[...] = heads[0:natural, 0:outputs]
    head_two[...] = heads[natural:, 0:outputs]

    @pl.when(section > 0)
    def _():
        each_unit(lambda u: patch_copy(u).wait_send())

    @pl.when(section < last)
    def _():
        each_unit(lambda u: hop(u).wait_send())

    @pl.when(section == last)
    def _():
        def finish(u):
            for target, step in film_targets:
                film_copy(u, target, step).wait_send()

        each_unit(finish)


def on_device(
    patches,
    clip_slot,
    w_qkv,
    w_out,
    w_up,
    w_down,
    norm_gains,
    level_one_weight,
    level_two_weight,
    head_weight,
):
    sections = lax.axis_size("section")
    shards = lax.axis_size("dp")
    rows, channels = patches.shape
    width = channels * sections
    unit_rows = UNIT_ROWS
    units = rows // unit_rows
    tubes_unit = unit_rows // PATCHES
    outputs = head_weight.shape[1]
    one_rows = rows // PATCHES // 2
    two_rows = one_rows // 2
    vmem = pl.BlockSpec(memory_space=pltpu.VMEM)
    anywhere = pl.BlockSpec(memory_space=pl.ANY)
    dma = pltpu.SemaphoreType.DMA
    return pl.pallas_call(
        functools.partial(kernel, sections, shards),
        out_shape=(
            jax.ShapeDtypeStruct((one_rows, outputs), F32),
            jax.ShapeDtypeStruct((two_rows, outputs), F32),
        ),
        in_specs=[anywhere, vmem] + [anywhere] * 4 + [vmem] + [anywhere] * 2 + [vmem],
        out_specs=(vmem, vmem),
        scratch_shapes=[
            pltpu.VMEM(w_qkv.shape[1:], BF16),
            pltpu.VMEM(w_out.shape[1:], BF16),
            pltpu.VMEM(w_up.shape[1:], BF16),
            pltpu.VMEM(w_down.shape[1:], BF16),
            pltpu.VMEM(level_one_weight.shape, BF16),
            pltpu.VMEM(level_two_weight.shape, BF16),
            pltpu.VMEM((sections, units, unit_rows, channels), BF16),
            pltpu.VMEM((units, unit_rows, width), BF16),
            pltpu.VMEM((units, unit_rows, width), BF16),
            pltpu.VMEM((units, sections, tubes_unit, channels), F32),
            pltpu.VMEM((shards, units, tubes_unit, channels), F32),
            pltpu.VMEM((sections, 3 * two_rows, channels), BF16),
            pltpu.VMEM((sections, 3 * two_rows, channels), BF16),
            pltpu.VMEM((sections, two_rows, channels), BF16),
            pltpu.VMEM((sections, two_rows, channels), BF16),
            pltpu.VMEM((3 * two_rows, 128), F32),
            pltpu.VMEM((sections, 3 * two_rows, 128), F32),
            dma((6,)),
            dma((units,)),
            dma((sections, units)),
            dma((units,)),
            dma((units,)),
            dma((units, sections, shards)),
            dma((shards, units)),
            dma((3, sections)),
            dma((3, sections)),
        ],
        compiler_params=pltpu.CompilerParams(
            collective_id=0, has_side_effects=True, vmem_limit_bytes=60 * 1024 * 1024
        ),
    )(
        patches,
        clip_slot.reshape(1, -1),
        w_qkv,
        w_out,
        w_up,
        w_down,
        norm_gains,
        level_one_weight,
        level_two_weight,
        head_weight,
    )


def solution(mesh):
    return jax.shard_map(
        on_device,
        mesh=mesh,
        in_specs=(
            P(("groups", "dp"), "section"),
            P("groups"),
            P("section", None, None),
            P("section", None, None),
            P("section", None, None),
            P("section", None, None),
            P("section", None, None),
            P(None, "section", None),
            P(None, "section", None),
            P("section", None),
        ),
        out_specs=(P(("groups", "dp"), None), P(("groups", "dp"), None)),
        check_vma=False,
    )
```

time: 557 us -> 79.7 us (0.14)
  matrix products: 158 us -> 0 us
  waiting for transfers between devices: 138 us -> 0 us
  starting transfers between devices: 105 us -> 0 us
  Pallas kernels: 0 us -> 74.6 us
  other arithmetic: 57.8 us -> 0 us
  local copies, waits for them, and re-layouts: 41 us -> 4.13 us
  blocking collectives: 36.7 us -> 0 us
  between operations: 13.9 us -> 0.64 us
    dot_general x85 -> x0, matrix products: 158 us -> none  [the longest x16 84.4 us: vit_layer(): jnp.dot(hidden, w_down, preferred_element_type=jnp.float32)]
    ppermute x20 -> x0, starting transfers between devices: 105 us -> none  [shifted(): lax.ppermute(value, axis, [(source, source + steps) for source in range(l...]
    psum x2 -> x0, waiting for transfers between devices: 92.2 us -> none  [the longest x1 60.7 us: broadcast(): return lax.psum(kept, axis)]
    pallas_call x0 -> x1, Pallas kernels: none -> 74.6 us  [on_device(): pl.pallas_call(functools.partial(kernel, sections, shards), out_shape=(ja...]
    slice x55 -> x0, local copies, waits for them, and re-layouts: 33.4 us -> none  [the longest x16 22.1 us: vit_layer(): normed_b = layer_norm(residual, gains[1]).astype(jnp.bfloat16)]
    all_gather x1 -> x0, waiting for transfers between devices: 25.7 us -> none  [on_device(): gathered = lax.all_gather(patches, 'section', axis=1, tiled=True)]
    dynamic_update_slice x19 -> x0, other arithmetic: 25.3 us -> none  [advance(): lax.dynamic_update_slice_in_dim(pooled, jnp.where(record_here, tube_means...]
    psum x2 -> x0, blocking collectives: 21.8 us -> none  [the longest x1 11.1 us: on_device(): head_one, head_two = lax.psum((head_one, head_two), 'section')]
  transfers between devices with their start and end apart: 23 -> 0, of which waited for: 23 -> 0; matrix products, arithmetic and copies ran while one was open for 0% -> 0% of each run, Pallas kernels for 0% -> 0%
where the time goes in v1:
time: 79.7 us; the launch traced here: 79.3 us
  Pallas kernels  74.6 us (94%)
  local copies, waits for them, and re-layouts  4.13 us (5%)
    pallas_call x1, Pallas kernels, on_device(): pl.pallas_call(functools.partial(kernel, sections, shards), out_shape=(ja...  74.6 us
    unnamed x2, local copies, waits for them, and re-layouts  2.74 us

profile of v1, /device:TPU:0, one launch (start us, length us, event | category | flops | bytes accessed | tf_op | source)
XLA Modules:
  0.0 79.3 jit_solution(10818795360982807443)
XLA Ops:
  0.6 1.4 %copy.12.head_weight = bf16[256,22]{1,0:T(8,128)(2,1)} copy(bf16[256,22]{0,1:T(8,128)(2,1)} %param.19) | data formatting | bytes 22528 | tf_op args[9]
  2.1 74.6 %shard_map.113 = (f32[32,22]{1,0:T(8,128)}, f32[16,22]{1,0:T(8,128)}) custom-call(bf16[1024,256]{1,0:T(8,128)(2,1)} %patches.1, s32[1,128]{1,0:T(1,128)} %bitcast.1, bf16[1,1024,1536]{2,1,0:T(8,128)(2,1)} %w_qkv.1, bf16[1,512,1024]{2,1,0:T(8,128)(2,1)} %w_out.1, bf16[1,1024,2048]{2,1,0:T(8,128)(2,1)} %w_up.1, bf16[1,2048,1024]{2,1,0:T(8,128)(2,1)} %w_down.1, ...), custom_call_target="tpu_custom_call" | custom-call | tf_op jit(solution)/shard_map/pallas_call | solution.py:425
  76.7 1.4 %copy.13 = f32[32,22]{0,1:T(8,128)} copy(f32[32,22]{1,0:T(8,128)} %get-tuple-element.2) | data formatting | bytes 5632 | tf_op jit(solution)/shard_map/pallas_call | solution.py:425
  78.0 1.3 %copy.15 = f32[16,22]{1,0:T(8,128)} copy(f32[16,22]{1,0:T(8,128)} %get-tuple-element.7) | data formatting | bytes 2816

commit v2 on v1

--- a/solution.py
+++ b/solution.py
@@ -37,6 +37,12 @@
 
 def gelu(values):
     return jax.nn.gelu(values, approximate=True)
+
+
+def gelu_rounded(values):
+    x = values.astype(BF16)
+    inner = x * (x * x * 0.035677408136300125 + 0.7978845608028654)
+    return x * (jnp.tanh(inner) * 0.5 + 0.5)
 
 
 def iota(shape, dim):
@@ -93,8 +99,7 @@
     one_weight,
     two_weight,
     head_weight,
-    head_one,
-    head_two,
+    heads,
     v_qkv,
     v_out,
     v_up,
@@ -143,7 +148,7 @@
             )
         )
     ]
-    for load in loads:
+    for load in loads[:4]:
         load.start()
 
     barrier = pltpu.get_barrier_semaphore()
@@ -250,14 +255,18 @@
 
         @pl.when(u == 0)
         def _():
-            loads[1].wait()
-            loads[2].wait()
-            loads[3].wait()
+            for load in loads[1:4]:
+                load.wait()
+            for load in loads[4:]:
+                load.start()
 
         residual = stream + dot(mixture, v_out[...])
         normed_b = layer_norm(residual, gains[0, 1:2]).astype(BF16)
+        ahead = dot(normed_b, v_up[:, :CHUNK])
         for start in range(0, hidden, CHUNK):
-            part = gelu(dot(normed_b, v_up[:, start : start + CHUNK])).astype(BF16)
+            part = gelu_rounded(ahead)
+            if start + CHUNK < hidden:
+                ahead = dot(normed_b, v_up[:, start + CHUNK : start + 2 * CHUNK])
             residual = residual + dot(part, v_down[start : start + CHUNK, :])
         result = residual.astype(BF16)
 
@@ -301,7 +310,7 @@
     position = TUB_CLIP * dot(slots, spread.astype(BF16))[0:1]
     position = position + (iota((1, tubes), 1) % TUB_CLIP).astype(F32)
 
-    two_rows = head_two.shape[0]
+    two_rows = heads.shape[0] // 3
     one_rows = 3 * two_rows
     row = iota((one_rows, 1), 0)
     level_index = 2 * (shard * two_rows + row % two_rows) + row // two_rows - 1
@@ -369,16 +378,14 @@
     order = (natural, one_rows)
     chosen = iota(order, 1) == (1 + iota(order, 0) % 2) * two_rows + iota(order, 0) // 2
     one_natural = dot(jnp.where(chosen, 1.0, 0.0).astype(BF16), one).astype(BF16)
-    outputs = head_weight.shape[1]
+    outputs = head_weight.shape[0]
     heads_out[...] = jnp.zeros(heads_out.shape, F32)
-    heads_out[0:natural, 0:outputs] = dot(one_natural, head_weight[...])
-    heads_out[natural:, 0:outputs] = dot(two, head_weight[...])
+    heads_out[0:natural, 0:outputs] = dot_nt(one_natural, head_weight[...])
+    heads_out[natural:, 0:outputs] = dot_nt(two, head_weight[...])
     arrivals = exchange(2, lambda target: heads_out, heads_in)
     heads_in[section] = heads_out[...]
     arrivals()
-    heads = total(heads_in)
-    head_one[...] = heads[0:natural, 0:outputs]
-    head_two[...] = heads[natural:, 0:outputs]
+    heads[...] = total(heads_in)
 
     @pl.when(section > 0)
     def _():
@@ -395,6 +402,12 @@
                 film_copy(u, target, step).wait_send()
 
         each_unit(finish)
+
+
+def split_heads(heads, head_one, head_two):
+    outputs, natural = head_one.shape
+    head_one[...] = heads[0:natural].T[0:outputs]
+    head_two[...] = heads[natural:, 0:outputs]
 
 
 def on_device(
@@ -422,14 +435,11 @@
     vmem = pl.BlockSpec(memory_space=pltpu.VMEM)
     anywhere = pl.BlockSpec(memory_space=pl.ANY)
     dma = pltpu.SemaphoreType.DMA
-    return pl.pallas_call(
+    heads = pl.pallas_call(
         functools.partial(kernel, sections, shards),
-        out_shape=(
-            jax.ShapeDtypeStruct((one_rows, outputs), F32),
-            jax.ShapeDtypeStruct((two_rows, outputs), F32),
-        ),
+        out_shape=jax.ShapeDtypeStruct((3 * two_rows, 128), F32),
         in_specs=[anywhere, vmem] + [anywhere] * 4 + [vmem] + [anywhere] * 2 + [vmem],
-        out_specs=(vmem, vmem),
+        out_specs=vmem,
         scratch_shapes=[
             pltpu.VMEM(w_qkv.shape[1:], BF16),
             pltpu.VMEM(w_out.shape[1:], BF16),
@@ -471,8 +481,18 @@
         norm_gains,
         level_one_weight,
         level_two_weight,
-        head_weight,
+        head_weight.T,
     )
+    head_one, head_two = pl.pallas_call(
+        split_heads,
+        out_shape=(
+            jax.ShapeDtypeStruct((outputs, one_rows), F32),
+            jax.ShapeDtypeStruct((two_rows, outputs), F32),
+        ),
+        in_specs=[vmem],
+        out_specs=(vmem, vmem),
+    )(heads)
+    return head_one.T, head_two
 
 
 def solution(mesh):

time: 79.7 us -> 70.5 us (0.88)
  Pallas kernels: 74.6 us -> 69.6 us
  local copies, waits for them, and re-layouts: 4.13 us -> 0 us
    pallas_call x1 -> x2, Pallas kernels: 74.6 us -> 69.6 us  [the longest x1 68.2 us: on_device(): pl.pallas_call(functools.partial(kernel, sections, shards), out_shape=jax...]
    unnamed x2 -> x0, local copies, waits for them, and re-layouts: 2.74 us -> none
    pallas_call x1 -> x0, local copies, waits for them, and re-layouts: 1.4 us -> none  [on_device(): pl.pallas_call(functools.partial(kernel, sections, shards), out_shape=(ja...]
where the time goes in v2:
time: 70.5 us; the launch traced here: 70.2 us
  Pallas kernels  69.6 us (99%)
    pallas_call x1, Pallas kernels, on_device(): pl.pallas_call(functools.partial(kernel, sections, shards), out_shape=jax...  68.2 us
    pallas_call x1, Pallas kernels, on_device(): pl.pallas_call(split_heads, out_shape=(jax.ShapeDtypeStruct((outputs, one...  1.41 us

profile of v2, /device:TPU:0, one launch (start us, length us, event | category | flops | bytes accessed | tf_op | source)
XLA Modules:
  0.0 70.2 jit_solution(7009017489771286676)
XLA Ops:
  0.6 68.2 %shard_map.113.heads = f32[48,128]{1,0:T(8,128)} custom-call(bf16[1024,256]{1,0:T(8,128)(2,1)} %patches.1, s32[1,128]{1,0:T(1,128)} %bitcast.4, bf16[1,1024,1536]{2,1,0:T(8,128)(2,1)} %w_qkv.1, bf16[1,512,1024]{2,1,0:T(8,128)(2,1)} %w_out.1, bf16[1,1024,2048]{2,1,0:T(8,128)(2,1)} %w_up.1, bf16[1,2048,1024]{2,1,0:T(8,128)(2,1)} %w_down.1, ...), custom_call_target="tpu_custom_call" | custom-call | tf_op jit(solution)/shard_map/pallas_call | solution.py:438
  68.8 1.4 %shard_map.114 = (f32[22,32]{1,0:T(8,128)}, f32[16,22]{1,0:T(8,128)}) custom-call(f32[48,128]{1,0:T(8,128)} %shard_map.113.heads), custom_call_target="tpu_custom_call" | custom-call | tf_op jit(solution)/shard_map/pallas_call | solution.py:486
